TPU v7x, 256 devices: a whole 4x4x8 slice. The times are simulated.
256 devices in a mesh: fsdp: 32 (over z_hi, x, y), ep: 8 (over z_lo, core).
Axes of the slice: x: 4, y: 4, z: 8 (z_hi: 2, z_lo: 4; z = z_hi * 4 + z_lo), core: 2. Of those that a mesh axis runs over, the one named last changes fastest.
Arguments:
- tokens: bfloat16 [32768, 2048], P(('fsdp', 'ep')), may hold values from -24 to 24
- routes: int32 [32768, 6], P(('fsdp', 'ep')), may hold values from 0 to 63, as said below
- route_weight: float32 [32768, 6], P(('fsdp', 'ep')), may hold values from 0.1 to 1
- w_in: bfloat16 [8, 2048, 2, 768], P('ep', 'fsdp'), may hold values from -0.125 to 0.125
- w_down: bfloat16 [8, 768, 2048], P('ep', 'fsdp'), may hold values from -0.21875 to 0.21875
- cotangent: bfloat16 [32768, 2048], P(('fsdp', 'ep')), may hold values from -6 to 6
Outputs:
- layer_out: bfloat16 [32768, 2048], P(('fsdp', 'ep'))
- grad_tokens: bfloat16 [32768, 2048], P(('fsdp', 'ep'))
- grad_in: float32 [8, 2048, 2, 768], P('ep', 'fsdp')
- grad_down: float32 [8, 768, 2048], P('ep', 'fsdp')
Inputs may be any that keep to these rules, and one draw needn't show every extreme that they name: `routes`: each row names 6 different experts. The rows of one device name each window expert 0 to 7 at most 32 times; in every draw every device names some window expert exactly 32 times, and for some index of fsdp one window expert is named exactly 32 times by each device with that index.
All inputs are finite; a program needn't handle non-finite values.
Results may differ from a plain program's by a relative error of at most 0.014.
Values may be sent and summed in bfloat16 or wider, within the bound.
A program may use at most 64 MiB of HBM per device.

v0:
```python
import jax
import jax.numpy as jnp
from jax import lax
from jax.sharding import PartitionSpec as P

D = 2048
FF = 768
CAP = 32


def contract_rows(left, right):
    return lax.dot_general(
        left, right, (((0,), (0,)), ((), ())), preferred_element_type=jnp.float32
    )


def contract_cols(left, right):
    return lax.dot_general(
        left, right, (((1,), (1,)), ((), ())), preferred_element_type=jnp.float32
    )


def local(tokens, routes, route_weight, w_in, w_down, cotangent):
    ep_width = lax.axis_size("ep")
    all_rows = ep_width * CAP
    expert_ids = jnp.arange(ep_width, dtype=jnp.int32)
    route_hits = routes[:, :, None] == expert_ids[None, None, :]
    member = jnp.any(route_hits, axis=1).astype(jnp.int32)
    route_coef = jnp.sum(jnp.where(route_hits, route_weight[:, :, None], 0.0), axis=1)
    slot_rank = jnp.cumsum(member, axis=0) - member
    slot_ids = jnp.arange(CAP, dtype=jnp.int32)
    slot_hits = (slot_rank.T[:, None, :] == slot_ids[None, :, None]) & (member.T[:, None, :] > 0)
    dispatch = slot_hits.astype(jnp.bfloat16)
    slot_coef = jnp.sum(jnp.where(slot_hits, route_coef.T[:, None, :], 0.0), axis=2)
    weighted_dispatch = jnp.where(slot_hits, route_coef.T[:, None, :], 0.0)
    send_x = jnp.einsum("est,td->esd", dispatch, tokens, preferred_element_type=jnp.float32).astype(
        jnp.bfloat16
    )
    dy_rows = jnp.einsum("est,td->esd", dispatch, cotangent, preferred_element_type=jnp.float32)
    send_dy = (dy_rows * slot_coef[:, :, None]).astype(jnp.bfloat16)
    full_in, full_down = (
        lax.all_gather(w_in[0], "fsdp", axis=0, tiled=True),
        lax.all_gather(w_down[0], "fsdp", axis=0, tiled=True),
    )
    flat_in = full_in.reshape(D, 2 * FF)
    recv_x = lax.all_to_all(send_x, "ep", split_axis=0, concat_axis=0, tiled=True)
    rows_x = recv_x.reshape(all_rows, D)
    gate_up = jnp.dot(rows_x, flat_in, preferred_element_type=jnp.float32)
    gate_vals = gate_up[:, :FF]
    up_vals = gate_up[:, FF:]
    sig_gate = jax.nn.sigmoid(gate_vals)
    act_vals = gate_vals * sig_gate
    hidden = (act_vals * up_vals).astype(jnp.bfloat16)
    out_rows = jnp.dot(hidden, full_down, preferred_element_type=jnp.float32).astype(jnp.bfloat16)
    out_rows = out_rows.reshape(ep_width, CAP, D)
    back_out = lax.all_to_all(out_rows, "ep", split_axis=0, concat_axis=0, tiled=True)
    recv_dy = lax.all_to_all(send_dy, "ep", split_axis=0, concat_axis=0, tiled=True)
    rows_dy = recv_dy.reshape(all_rows, D)
    grad_hidden = contract_cols(rows_dy, full_down)
    grad_gate = grad_hidden * up_vals * sig_gate * (1.0 + gate_vals * (1.0 - sig_gate))
    grad_up = grad_hidden * act_vals
    grad_gu = jnp.concatenate([grad_gate, grad_up], axis=1).astype(jnp.bfloat16)
    input_rows = contract_cols(grad_gu, flat_in).astype(jnp.bfloat16).reshape(ep_width, CAP, D)
    term_in = contract_rows(rows_x, grad_gu)
    term_down = contract_rows(hidden, rows_dy)
    grad_in, grad_down = (
        lax.psum_scatter(
            term_in.astype(jnp.bfloat16), "fsdp", scatter_dimension=0, tiled=True
        ).astype(jnp.float32),
        lax.psum_scatter(
            term_down.astype(jnp.bfloat16), "fsdp", scatter_dimension=0, tiled=True
        ).astype(jnp.float32),
    )
    back_dx = lax.all_to_all(input_rows, "ep", split_axis=0, concat_axis=0, tiled=True)
    mixed_sum = jnp.einsum(
        "est,esd->td",
        weighted_dispatch,
        back_out.astype(jnp.float32),
        preferred_element_type=jnp.float32,
    )
    grad_sum = jnp.einsum("est,esd->td", dispatch, back_dx, preferred_element_type=jnp.float32)
    layer_out = mixed_sum.astype(jnp.bfloat16)
    grad_tokens = grad_sum.astype(jnp.bfloat16)
    grad_in = grad_in.reshape(w_in.shape)
    grad_down = grad_down.reshape(w_down.shape)
    return (layer_out, grad_tokens, grad_in, grad_down)


def solution(mesh):
    in_specs = (
        P(("fsdp", "ep"), None),
        P(("fsdp", "ep"), None),
        P(("fsdp", "ep"), None),
        P("ep", "fsdp", None, None),
        P("ep", "fsdp", None),
        P(("fsdp", "ep"), None),
    )
    out_specs = (
        P(("fsdp", "ep"), None),
        P(("fsdp", "ep"), None),
        P("ep", "fsdp", None, None),
        P("ep", "fsdp", None),
    )
    return jax.shard_map(local, mesh=mesh, in_specs=in_specs, out_specs=out_specs, check_vma=False)
```

profile of v0, /device:TPU:1, one launch (start us, length us, event | category | flops | bytes accessed | tf_op | source)
XLA Modules:
  0.0 798.5 jit_solution(17378542734916853659)
XLA Ops:
  9.9 1.5 convolution_convert_fusion.2
  11.3 7.4 all-to-all-start
  18.9 1.5 fusion.4
  20.4 26.9 %all-to-all-done = bf16[8,32,2048]{2,1,0:T(8,128)(2,1)S(1)} async-done(((bf16[8,32,2048]{2,1,0:T(8,128)(2,1)}), bf16[8,32,2048]{2,1,0:T(8,128)(2,1)S(1)}, u32[]{:S(2)}, u32[]{:S(2)}) %all-to-all-start) | async-done | bytes 1048608 | tf_op jit(solution)/shard_map/all_to_all | solution.py:46
  47.2 4.3 all-to-all-start.2
  51.6 108.5 %all-gather.5.cloned.1.call-done = bf16[1,2048,2,768]{3,2,0,1:T(2,128)(2,1)} async-done(((bf16[1,64,2,768]{3,2,0,1:T(2,128)(2,1)}), bf16[1,2048,2,768]{3,2,0,1:T(2,128)(2,1)}) %all-gather.5.cloned.1.call-update) | async-done | bytes 6291472 | tf_op jit(solution)/shard_map/all_gather | solution.py:42
  160.1 4.1 copy.23
  164.2 2.7 copy-done.1
  166.9 2.9 fusion.33
  169.8 88.4 %all-gather.7.cloned.1.call-done = bf16[1,768,2048]{2,1,0:T(8,128)(2,1)} async-done(((bf16[1,24,2048]{2,1,0:T(8,128)(2,1)}), bf16[1,768,2048]{2,1,0:T(8,128)(2,1)}) %all-gather.7.cloned.1.call-update) | async-done | bytes 3145744 | tf_op jit(solution)/shard_map/all_gather | solution.py:43
  258.2 4.3 multiply_convert_fusion.1
  262.5 2.7 convolution_convert_fusion.1
  266.2 4.5 convolution_convert_fusion
  270.7 3.9 fusion.5
  274.6 5.8 all-to-all-start.1
  280.4 5.7 convolution_convert_fusion.3
  286.0 22.8 %all-to-all-done.1 = bf16[8,32,2048]{2,1,0:T(8,128)(2,1)S(1)} async-done(((bf16[8,32,2048]{2,1,0:T(8,128)(2,1)}), bf16[8,32,2048]{2,1,0:T(8,128)(2,1)S(1)}, u32[]{:S(2)}, u32[]{:S(2)}) %all-to-all-start.1) | async-done | bytes 1048608 | tf_op jit(solution)/shard_map/all_to_all | solution.py:56
  308.8 4.3 all-to-all-start.3
  314.3 27.2 %all-to-all-done.3 = bf16[8,32,2048]{2,1,0:T(8,128)(2,1)S(1)} async-done(((bf16[8,32,2048]{2,1,0:T(8,128)(2,1)}), bf16[8,32,2048]{2,1,0:T(8,128)(2,1)S(1)}, u32[]{:S(2)}, u32[]{:S(2)}) %all-to-all-start.3) | async-done | bytes 1048608 | tf_op jit(solution)/shard_map/all_to_all | solution.py:74
  341.5 1.1 fusion.9
  342.7 176.0 %reduce-scatter.5.cloned.1.call-done = bf16[24,2048]{1,0:T(8,128)(2,1)} async-done(((bf16[768,2048]{1,0:T(8,128)(2,1)}), bf16[24,2048]{1,0:T(8,128)(2,1)}) %reduce-scatter.5.cloned.1.call-update) | async-done | bytes 98320 | tf_op jit(solution)/shard_map/reduce_scatter | solution.py:70
  518.7 1.6 bitcast_convert_fusion
  520.3 269.7 %reduce-scatter.3.cloned.1.call-done = bf16[64,1536]{1,0:T(8,128)(2,1)} async-done(((bf16[2048,1536]{1,0:T(8,128)(2,1)}), bf16[64,1536]{1,0:T(8,128)(2,1)}) %reduce-scatter.3.cloned.1.call-update) | async-done | bytes 196624 | tf_op jit(solution)/shard_map/reduce_scatter | solution.py:67
  790.0 1.9 reshape.52
  (30 shorter events, 4.9 us)
Async XLA Ops:
  7.2 2.7 copy-start
  7.2 11.5 %copy-start.4 = (s32[128,6]{0,1:T(8,128)S(1)}, s32[128,6]{0,1:T(8,128)}, u32[]{:S(2)}) copy-start(s32[128,6]{0,1:T(8,128)} %param.7) | copy-start | bytes 9220
  7.2 11.5 %copy-start.5 = (f32[128,6]{0,1:T(8,128)S(1)}, f32[128,6]{0,1:T(8,128)}, u32[]{:S(2)}) copy-start(f32[128,6]{0,1:T(8,128)} %param.8) | copy-start | bytes 9220
  7.2 11.6 %copy-start.2 = (bf16[128,2048]{1,0:T(8,128)(2,1)S(1)}, bf16[128,2048]{1,0:T(8,128)(2,1)}, u32[]{:S(2)}) copy-start(bf16[128,2048]{1,0:T(8,128)(2,1)} %param.11) | copy-start | bytes 1572868
  7.2 152.9 %all-gather.5.cloned.1.call-start = ((), (), s32[]{:S(2)}) async-start(), calls=%async_computation.8 | async-start | bytes 6488064 | tf_op jit(solution)/shard_map/all_gather | solution.py:42
  7.9 250.3 %all-gather.7.cloned.1.call-start = ((), (), s32[]{:S(2)}) async-start(), calls=%async_computation.9 | async-start | bytes 3244032 | tf_op jit(solution)/shard_map/all_gather | solution.py:43
  11.3 35.9 %all-to-all-start = ((bf16[8,32,2048]{2,1,0:T(8,128)(2,1)}), bf16[8,32,2048]{2,1,0:T(8,128)(2,1)S(1)}, u32[]{:S(2)}, u32[]{:S(2)}) async-start(bf16[8,32,2048]{2,1,0:T(8,128)(2,1)} %convolution_convert_fusion.2), calls=%async_computation | async-start | bytes 2097152 | tf_op jit(solution)/shard_map/all_to_all | solution.py:46
  47.2 122.6 %all-to-all-start.2 = ((bf16[8,32,2048]{2,1,0:T(8,128)(2,1)}), bf16[8,32,2048]{2,1,0:T(8,128)(2,1)S(1)}, u32[]{:S(2)}, u32[]{:S(2)}) async-start(bf16[8,32,2048]{2,1,0:T(8,128)(2,1)} %fusion.4), calls=%async_computation.2 | async-start | bytes 2097152 | tf_op jit(solution)/shard_map/all_to_all | solution.py:57
  51.6 467.1 %reduce-scatter.5.cloned.1.call-start = ((), (), s32[]{:S(2)}) async-start(), calls=%async_computation.7 | async-start | bytes 3244032 | tf_op jit(solution)/shard_map/reduce_scatter | solution.py:70
  164.2 2.7 copy-start.1
  265.2 1.0 copy-start.3
  265.2 524.8 %reduce-scatter.3.cloned.1.call-start = ((), (), s32[]{:S(2)}) async-start(), calls=%async_computation.6 | async-start | bytes 6488064 | tf_op jit(solution)/shard_map/reduce_scatter | solution.py:67
  274.6 34.2 %all-to-all-start.1 = ((bf16[8,32,2048]{2,1,0:T(8,128)(2,1)}), bf16[8,32,2048]{2,1,0:T(8,128)(2,1)S(1)}, u32[]{:S(2)}, u32[]{:S(2)}) async-start(bf16[8,32,2048]{2,1,0:T(8,128)(2,1)} %bitcast.7), calls=%async_computation.1 | async-start | bytes 2097152 | tf_op jit(solution)/shard_map/all_to_all | solution.py:56
  308.8 32.7 %all-to-all-start.3 = ((bf16[8,32,2048]{2,1,0:T(8,128)(2,1)}), bf16[8,32,2048]{2,1,0:T(8,128)(2,1)S(1)}, u32[]{:S(2)}, u32[]{:S(2)}) async-start(bf16[8,32,2048]{2,1,0:T(8,128)(2,1)} %bitcast.57), calls=%async_computation.3 | async-start | bytes 2097152 | tf_op jit(solution)/shard_map/all_to_all | solution.py:74
Sparse Core Ops, SparseCore 0:
  11.4 148.5 all-gather.4
  163.5 94.6 all-gather.6
  265.3 253.3 reduce-scatter.4
  525.0 264.9 reduce-scatter.2
where the time goes:
time: 799 us; the launch traced here: 798 us
  waiting for transfers between devices  721 us (90%)
  matrix products  29.2 us (4%)
  starting transfers between devices  22 us (3%)
  between operations  13.8 us (2%)
  local copies, waits for them, and re-layouts  9.89 us (1%)
    reduce_scatter x1, waiting for transfers between devices, local(): lax.psum_scatter(term_in.astype(jnp.bfloat16), 'fsdp', scatter_dimension=...  270 us
    reduce_scatter x1, waiting for transfers between devices, local(): lax.psum_scatter(term_down.astype(jnp.bfloat16), 'fsdp', scatter_dimensio...  176 us
    all_gather x1, waiting for transfers between devices, local(): lax.all_gather(w_in[0], 'fsdp', axis=0, tiled=True)  108 us
    all_gather x1, waiting for transfers between devices, local(): lax.all_gather(w_down[0], 'fsdp', axis=0, tiled=True)  88.4 us
    all_to_all x1, waiting for transfers between devices, local(): lax.all_to_all(input_rows, 'ep', split_axis=0, concat_axis=0, tiled=True)  27.2 us
    all_to_all x1, waiting for transfers between devices, local(): lax.all_to_all(send_x, 'ep', split_axis=0, concat_axis=0, tiled=True)  26.9 us
    all_to_all x1, waiting for transfers between devices, local(): lax.all_to_all(out_rows, 'ep', split_axis=0, concat_axis=0, tiled=True)  22.8 us
  transfers between devices with their start and end apart: 8, of which 7 were waited for; matrix products, arithmetic and copies ran while one was open for 4% of the time, Pallas kernels for 0%

commit v1 on v0

--- a/solution.py
+++ b/solution.py
@@ -6,6 +6,13 @@
 D = 2048
 FF = 768
 CAP = 32
+
+
+def all_by_exchange(x, mesh_axis, along):
+    count = lax.axis_size(mesh_axis)
+    parts = jnp.stack([x for _ in range(count)])
+    parts = lax.all_to_all(parts, mesh_axis, split_axis=0, concat_axis=0)
+    return jnp.concatenate(parts, axis=along)
 
 
 def contract_rows(left, right):
@@ -40,7 +47,7 @@
     send_dy = (dy_rows * slot_coef[:, :, None]).astype(jnp.bfloat16)
     full_in, full_down = (
         lax.all_gather(w_in[0], "fsdp", axis=0, tiled=True),
-        lax.all_gather(w_down[0], "fsdp", axis=0, tiled=True),
+        all_by_exchange(w_down[0], "fsdp", 0),
     )
     flat_in = full_in.reshape(D, 2 * FF)
     recv_x = lax.all_to_all(send_x, "ep", split_axis=0, concat_axis=0, tiled=True)

time: 799 us -> 770 us (0.964)
  waiting for transfers between devices: 721 us -> 636 us
  blocking collectives: 0 us -> 40.1 us
  starting transfers between devices: 22 us -> 36.3 us
    all_gather x1 -> x0, waiting for transfers between devices: 88.4 us -> none  [local(): lax.all_gather(w_down[0], 'fsdp', axis=0, tiled=True)]
    all_to_all x0 -> x1, blocking collectives: none -> 40.1 us  [local(): lax.all_to_all(send_x, 'ep', split_axis=0, concat_axis=0, tiled=True)]
    all_to_all x1, waiting for transfers between devices: 0.01 us -> 28.2 us  [local(): lax.all_to_all(send_dy, 'ep', split_axis=0, concat_axis=0, tiled=True)]
    all_gather x1, waiting for transfers between devices: 108 us -> 84.8 us  [local(): lax.all_gather(w_in[0], 'fsdp', axis=0, tiled=True)]
  transfers between devices with their start and end apart: 8 -> 7, of which waited for: 7 -> 7; matrix products, arithmetic and copies ran while one was open for 4% -> 4% of each run, Pallas kernels for 0% -> 0%
where the time goes in v1:
time: 770 us
  waiting for transfers between devices  636 us (83%)
  blocking collectives  40.1 us (5%)
  starting transfers between devices  36.3 us (5%)
  matrix products  28.8 us (4%)
  between operations  13.8 us (2%)
  local copies, waits for them, and re-layouts  11 us (1%)
    reduce_scatter x1, waiting for transfers between devices, local(): lax.psum_scatter(term_in.astype(jnp.bfloat16), 'fsdp', scatter_dimension=...  270 us
    reduce_scatter x1, waiting for transfers between devices, local(): lax.psum_scatter(term_down.astype(jnp.bfloat16), 'fsdp', scatter_dimensio...  182 us
    all_gather x1, waiting for transfers between devices, local(): lax.all_gather(w_in[0], 'fsdp', axis=0, tiled=True)  84.8 us
    all_to_all x1, blocking collectives, local(): lax.all_to_all(send_x, 'ep', split_axis=0, concat_axis=0, tiled=True)  40.1 us
    all_to_all x1, waiting for transfers between devices, local(): lax.all_to_all(send_dy, 'ep', split_axis=0, concat_axis=0, tiled=True)  28.2 us
    all_to_all x1, waiting for transfers between devices, local(): lax.all_to_all(input_rows, 'ep', split_axis=0, concat_axis=0, tiled=True)  27.9 us
    all_to_all x1, waiting for transfers between devices, local(): lax.all_to_all(out_rows, 'ep', split_axis=0, concat_axis=0, tiled=True)  22.5 us
    all_to_all x1, waiting for transfers between devices, all_by_exchange(): parts = lax.all_to_all(parts, mesh_axis, split_axis=0, concat_axis=0)  20.3 us
  transfers between devices with their start and end apart: 7, of which 7 were waited for; matrix products, arithmetic and copies ran while one was open for 4% of the time, Pallas kernels for 0%

profile of v1, /device:TPU:1, one launch (start us, length us, event | category | flops | bytes accessed | tf_op | source)
XLA Modules:
  0.0 769.5 jit_solution(8842844460601253918)
XLA Ops:
  9.9 1.4 fusion
  11.4 7.5 all-to-all-start.3
  19.3 28.2 %all-to-all-done.3 = bf16[8,32,2048]{2,1,0:T(8,128)(2,1)} async-done(((bf16[8,32,2048]{2,1,0:T(8,128)(2,1)}), bf16[8,32,2048]{2,1,0:T(8,128)(2,1)}, u32[]{:S(2)}, u32[]{:S(2)}) %all-to-all-start.3) | async-done | bytes 1048608 | tf_op jit(solution)/shard_map/all_to_all | solution.py:64
  47.5 40.1 %all_to_all.25 = bf16[8,32,2048]{2,1,0:T(8,128)(2,1)S(1)} all-to-all(bf16[8,32,2048]{2,1,0:T(8,128)(2,1)S(1)} %convolution_convert_fusion.2), channel_id=1, replica_groups=mesh['fsdp'=32,'ep'=8] {'ep'}, dimensions={0} | all-to-all | bytes 2097152 | tf_op jit(solution)/shard_map/all_to_all | solution.py:53
  87.6 2.1 stack.3
  89.7 12.0 %all-to-all-start.1 = ((bf16[32,24,2048]{2,1,0:T(8,128)(2,1)}), bf16[32,24,2048]{2,1,0:T(8,128)(2,1)}, u32[]{:S(2)}, u32[]{:S(2)}) async-start(bf16[32,24,2048]{2,1,0:T(8,128)(2,1)} %stack.3), calls=%async_computation.1 | async-start | bytes 6291456 | tf_op jit(solution)/shard_map/all_to_all | solution.py:14
  101.8 84.8 %all-gather.3.cloned.1.call-done = bf16[1,2048,2,768]{3,2,0,1:T(2,128)(2,1)} async-done(((bf16[1,64,2,768]{3,2,0,1:T(2,128)(2,1)}), bf16[1,2048,2,768]{3,2,0,1:T(2,128)(2,1)}) %all-gather.3.cloned.1.call-update) | async-done | bytes 6291472 | tf_op jit(solution)/shard_map/all_gather | solution.py:49
  186.6 4.1 copy.23
  190.8 2.6 copy-done.1
  193.4 2.9 fusion.26
  196.3 20.3 %all-to-all-done.1 = bf16[32,24,2048]{2,1,0:T(8,128)(2,1)} async-done(((bf16[32,24,2048]{2,1,0:T(8,128)(2,1)}), bf16[32,24,2048]{2,1,0:T(8,128)(2,1)}, u32[]{:S(2)}, u32[]{:S(2)}) %all-to-all-start.1) | async-done | bytes 3145760 | tf_op jit(solution)/shard_map/all_to_all | solution.py:14
  216.6 3.9 multiply_convert_fusion.1
  220.5 3.9 convolution_convert_fusion.1
  224.5 4.5 convolution_convert_fusion
  229.0 3.9 convolution_convert_fusion.4
  232.8 12.2 %all-to-all-start.2 = ((bf16[8,32,2048]{2,1,0:T(8,128)(2,1)}), bf16[8,32,2048]{2,1,0:T(8,128)(2,1)S(1)}, u32[]{:S(2)}, u32[]{:S(2)}) async-start(bf16[8,32,2048]{2,1,0:T(8,128)(2,1)} %bitcast.8), calls=%async_computation.2 | async-start | bytes 2097152 | tf_op jit(solution)/shard_map/all_to_all | solution.py:63
  245.0 5.6 convolution_convert_fusion.3
  250.6 22.5 %all-to-all-done.2 = bf16[8,32,2048]{2,1,0:T(8,128)(2,1)S(1)} async-done(((bf16[8,32,2048]{2,1,0:T(8,128)(2,1)}), bf16[8,32,2048]{2,1,0:T(8,128)(2,1)S(1)}, u32[]{:S(2)}, u32[]{:S(2)}) %all-to-all-start.2) | async-done | bytes 1048608 | tf_op jit(solution)/shard_map/all_to_all | solution.py:63
  273.2 4.5 all-to-all-start.4
  278.8 27.9 %all-to-all-done.4 = bf16[8,32,2048]{2,1,0:T(8,128)(2,1)S(1)} async-done(((bf16[8,32,2048]{2,1,0:T(8,128)(2,1)}), bf16[8,32,2048]{2,1,0:T(8,128)(2,1)S(1)}, u32[]{:S(2)}, u32[]{:S(2)}) %all-to-all-start.4) | async-done | bytes 1048608 | tf_op jit(solution)/shard_map/all_to_all | solution.py:81
  307.8 182.1 %reduce-scatter.5.cloned.1.call-done = bf16[24,2048]{1,0:T(8,128)(2,1)} async-done(((bf16[768,2048]{1,0:T(8,128)(2,1)}), bf16[24,2048]{1,0:T(8,128)(2,1)}) %reduce-scatter.5.cloned.1.call-update) | async-done | bytes 98320 | tf_op jit(solution)/shard_map/reduce_scatter | solution.py:77
  489.9 1.6 bitcast_convert_fusion
  491.5 269.6 %reduce-scatter.3.cloned.1.call-done = bf16[64,1536]{1,0:T(8,128)(2,1)} async-done(((bf16[2048,1536]{1,0:T(8,128)(2,1)}), bf16[64,1536]{1,0:T(8,128)(2,1)}) %reduce-scatter.3.cloned.1.call-update) | async-done | bytes 196624 | tf_op jit(solution)/shard_map/reduce_scatter | solution.py:74
  761.1 1.9 reshape.57
  (25 shorter events, 5.6 us)
Async XLA Ops:
  7.2 2.8 copy-start
  7.2 11.7 %copy-start.2 = (bf16[128,2048]{1,0:T(8,128)(2,1)S(1)}, bf16[128,2048]{1,0:T(8,128)(2,1)}, u32[]{:S(2)}) copy-start(bf16[128,2048]{1,0:T(8,128)(2,1)} %param.6) | copy-start | bytes 1572868
  7.2 179.4 %all-gather.3.cloned.1.call-start = ((), (), s32[]{:S(2)}) async-start(), calls=%async_computation.9 | async-start | bytes 6488064 | tf_op jit(solution)/shard_map/all_gather | solution.py:49
  11.4 76.2 %copy-start.3 = (bf16[1,24,2048]{2,1,0:T(8,128)(2,1)S(1)}, bf16[1,24,2048]{2,1,0:T(8,128)(2,1)}, u32[]{:S(2)}) copy-start(bf16[1,24,2048]{2,1,0:T(8,128)(2,1)} %param.10) | copy-start | bytes 294916
  11.4 36.2 %all-to-all-start.3 = ((bf16[8,32,2048]{2,1,0:T(8,128)(2,1)}), bf16[8,32,2048]{2,1,0:T(8,128)(2,1)}, u32[]{:S(2)}, u32[]{:S(2)}) async-start(bf16[8,32,2048]{2,1,0:T(8,128)(2,1)} %fusion), calls=%async_computation.3 | async-start | bytes 2097152 | tf_op jit(solution)/shard_map/all_to_all | solution.py:64
  89.7 126.9 %all-to-all-start.1 = ((bf16[32,24,2048]{2,1,0:T(8,128)(2,1)}), bf16[32,24,2048]{2,1,0:T(8,128)(2,1)}, u32[]{:S(2)}, u32[]{:S(2)}) async-start(bf16[32,24,2048]{2,1,0:T(8,128)(2,1)} %stack.3), calls=%async_computation.1 | async-start | bytes 6291456 | tf_op jit(solution)/shard_map/all_to_all | solution.py:14
  101.7 388.2 %reduce-scatter.5.cloned.1.call-start = ((), (), s32[]{:S(2)}) async-start(), calls=%async_computation.8 | async-start | bytes 3244032 | tf_op jit(solution)/shard_map/reduce_scatter | solution.py:77
  190.7 2.6 copy-start.1
  224.4 536.7 %reduce-scatter.3.cloned.1.call-start = ((), (), s32[]{:S(2)}) async-start(), calls=%async_computation.7 | async-start | bytes 6488064 | tf_op jit(solution)/shard_map/reduce_scatter | solution.py:74
  232.8 40.3 %all-to-all-start.2 = ((bf16[8,32,2048]{2,1,0:T(8,128)(2,1)}), bf16[8,32,2048]{2,1,0:T(8,128)(2,1)S(1)}, u32[]{:S(2)}, u32[]{:S(2)}) async-start(bf16[8,32,2048]{2,1,0:T(8,128)(2,1)} %bitcast.8), calls=%async_computation.2 | async-start | bytes 2097152 | tf_op jit(solution)/shard_map/all_to_all | solution.py:63
  273.2 33.5 %all-to-all-start.4 = ((bf16[8,32,2048]{2,1,0:T(8,128)(2,1)}), bf16[8,32,2048]{2,1,0:T(8,128)(2,1)S(1)}, u32[]{:S(2)}, u32[]{:S(2)}) async-start(bf16[8,32,2048]{2,1,0:T(8,128)(2,1)} %bitcast.50), calls=%async_computation.4 | async-start | bytes 2097152 | tf_op jit(solution)/shard_map/all_to_all | solution.py:81
Sparse Core Ops, SparseCore 0:
  11.4 175.1 all-gather.2
  224.5 265.3 reduce-scatter.4
  496.4 264.6 reduce-scatter.2
